TPU v7x, 256 devices: a whole 4x4x8 slice. The times are simulated.
256 devices in a mesh: dp: 8 (over z), seq: 32 (over x, y, core).
Axes of the slice: x: 4, y: 4, z: 8, core: 2. Of those that a mesh axis runs over, the one named last changes fastest.
Arguments:
- values_in: bfloat16 [8, 4096, 2048], P('dp', 'seq'), may hold values from -6 to 6
- input_proj: bfloat16 [8, 4096, 128], P('dp', 'seq'), may hold values from -0.5 to 0.5
- output_proj: bfloat16 [8, 4096, 128], P('dp', 'seq'), may hold values from -0.09375 to 0.09375
- log_decay: float32 [8, 32, 4096], P('dp', None, 'seq'), may hold values from -1 to 0, as said below
- doc_lengths: int32 [8, 8], P('dp'), may hold values from 1 to 2048, 4096 in all within a row
- skip_gain: float32 [32], replicated, may hold values from 0.5 to 1.5
- out_cotangent: bfloat16 [8, 4096, 2048], P('dp', 'seq'), may hold values from -6 to 6
Outputs:
- mixed_out: bfloat16 [8, 4096, 2048], P('dp', 'seq')
- values_grad: bfloat16 [8, 4096, 2048], P('dp', 'seq')
- input_grad: float32 [8, 4096, 128], P('dp', 'seq')
- output_grad: float32 [8, 4096, 128], P('dp', 'seq')
- decay_grad: float32 [8, 32, 4096], P('dp', None, 'seq')
- skip_grad: float32 [32], replicated
Inputs may be any that keep to these rules, and one draw needn't show every extreme that they name: `doc_lengths`: one row lists the documents of one sequence in order and sums to 4096. `log_decay`: negative log decay of each head at each token.
All inputs are finite; a program needn't handle non-finite values.
Results may differ from a plain program's by a relative error of at most 0.0056.
Values sent between devices are 32-bit elements; how exact they have to be, the bound alone decides.
No kernel may reach another device: no remote copies, remote signals or barrier semaphores. Data moves between devices by JAX's collectives and lax.ppermute only.
A program may use at most 128 MiB of HBM per device.

v0:
```python
import functools
import jax
import jax.numpy as jnp
from jax import lax
from jax.sharding import Mesh
from jax.sharding import PartitionSpec as P

SEQ = ("seq_0", "seq_1", "seq_2")
DP_SEQ = ("dp", "seq_0", "seq_1", "seq_2")


def in_one_piece(arrays, axis, split_dim, concat_dim, along):
    ends, at = ([], 0)
    for a in arrays[:-1]:
        at += a.shape[along]
        ends.append(at)
    both = jnp.concatenate(arrays, axis=along)
    return tuple(
        jnp.split(
            lax.all_to_all(both, axis, split_axis=split_dim, concat_axis=concat_dim, tiled=True),
            ends,
            axis=along,
        )
    )


def one_axis_at_a_time(x, axes):
    return functools.reduce(lax.psum, axes, x)


def product(form, left_side, right_side):
    return jnp.einsum(form, left_side, right_side, preferred_element_type=jnp.float32)


def block_stats(log_rows, resets):
    log_cum = jnp.cumsum(log_rows, axis=1)
    seg_count = jnp.cumsum(resets)
    log_end = log_cum[:, -1:]
    count_end = seg_count[-1]
    carry_gain = jnp.exp(log_end[:, 0]) * (count_end == 0).astype(jnp.float32)
    weight_end = jnp.exp(log_end - log_cum) * (seg_count == count_end).astype(jnp.float32)[None, :]
    weight_start = jnp.exp(log_cum) * (seg_count == 0).astype(jnp.float32)[None, :]
    return (log_cum, seg_count, carry_gain, weight_end, weight_start)


def head_scale(values, factors):
    row_count, inner_width = values.shape
    head_count = factors.shape[0]
    shaped = values.reshape(row_count, head_count, inner_width // head_count)
    return (shaped * factors.T[:, :, None]).reshape(row_count, inner_width)


def head_dot(left_side, right_side, head_count):
    row_count = left_side.shape[0]
    joined = left_side.astype(jnp.float32) * right_side.astype(jnp.float32)
    return jnp.sum(joined.reshape(row_count, head_count, -1), axis=2).T


def finish_block(
    values,
    input_rows,
    output_rows,
    grads_in,
    resets,
    skip_gain,
    stats,
    weighted_values,
    weighted_grads,
    state_in,
    adjoint_in,
):
    log_cum, seg_count, carry_gain, weight_end, weight_start = stats
    head_count = log_cum.shape[0]
    row_count, inner_width = values.shape
    head_dim = inner_width // head_count
    state_half = state_in.astype(jnp.bfloat16)
    adjoint_half = adjoint_in.astype(jnp.bfloat16)
    state_read = product("ln,in->li", output_rows, state_half)
    adjoint_read = product("ln,in->li", input_rows, adjoint_half)
    scores = product("tn,sn->ts", output_rows, input_rows)
    position = jnp.arange(row_count, dtype=jnp.int32)
    causal = (position[None, :] <= position[:, None]) & (seg_count[None, :] == seg_count[:, None])
    group_size = min(4, head_count)
    outs_within = []
    outs_back = []
    grad_parts = []
    grad_scores = jnp.zeros((row_count, row_count), jnp.float32)
    for block_index in range(head_count // group_size):
        first_head = block_index * group_size
        low_col = first_head * head_dim
        high_col = (first_head + group_size) * head_dim
        value_group = values[:, low_col:high_col].reshape(row_count, group_size, head_dim)
        grad_group = grads_in[:, low_col:high_col].reshape(row_count, group_size, head_dim)
        log_group = log_cum[first_head : first_head + group_size]
        log_gap = log_group[:, :, None] - log_group[:, None, :]
        decay_mat = jnp.exp(jnp.where(causal[None], log_gap, -jnp.inf))
        weighted = scores[None] * decay_mat
        mix_half = weighted.astype(jnp.bfloat16)
        outs_within.append(product("gts,sgp->tgp", mix_half, value_group).reshape(row_count, -1))
        outs_back.append(product("gts,tgp->sgp", mix_half, grad_group).reshape(row_count, -1))
        grad_mix = product("tgp,sgp->gts", grad_group, value_group)
        sensitivity = grad_mix * weighted
        grad_parts.append(jnp.sum(sensitivity, axis=2) - jnp.sum(sensitivity, axis=1))
        grad_scores = grad_scores + jnp.sum(grad_mix * decay_mat, axis=0)
    within_out = jnp.concatenate(outs_within, axis=1)
    back_part = jnp.concatenate(outs_back, axis=1)
    grad_cum = jnp.concatenate(grad_parts, axis=0)
    skip_rows = jnp.repeat(skip_gain, head_dim)[None, :]
    mixed = (within_out + head_scale(state_read, weight_start) + skip_rows * values).astype(
        jnp.bfloat16
    )
    values_grad = (back_part + head_scale(adjoint_read, weight_end) + skip_rows * grads_in).astype(
        jnp.bfloat16
    )
    grad_start = head_dot(grads_in, state_read, head_count)
    grad_end = head_dot(values, adjoint_read, head_count)
    grad_gain = jnp.sum((state_in * adjoint_in).reshape(head_count, -1), axis=1)
    end_total = jnp.sum(weight_end * grad_end, axis=1) + carry_gain * grad_gain
    grad_cum = grad_cum + weight_start * grad_start - weight_end * grad_end
    grad_cum = grad_cum.at[:, -1].add(end_total)
    decay_raw = (
        jnp.flip(jnp.cumsum(jnp.flip(grad_cum, 1), axis=1), 1)
        * (1 - resets).astype(jnp.float32)[None, :]
    )
    grad_half = grad_scores.astype(jnp.bfloat16)
    input_raw = product("ts,tn->sn", grad_half, output_rows) + product(
        "li,in->ln", weighted_values, adjoint_half
    )
    output_raw = product("ts,sn->tn", grad_half, input_rows) + product(
        "li,in->ln", weighted_grads, state_half
    )
    skip_part = jnp.sum(head_dot(grads_in, values, head_count), axis=1)
    return (mixed, values_grad, input_raw, output_raw, decay_raw, skip_part)


def body(values_in, input_proj, output_proj, log_decay, doc_lengths, skip_gain, out_cotangent):
    values = values_in[0]
    input_rows = input_proj[0]
    output_rows = output_proj[0]
    grads_in = out_cotangent[0]
    log_rows = log_decay[0]
    row_count, inner_width = values.shape
    head_count = log_rows.shape[0]
    head_dim = inner_width // head_count
    state_width = input_rows.shape[1]
    shards = lax.axis_size(SEQ)
    position = lax.axis_index(SEQ) * row_count + jnp.arange(row_count, dtype=jnp.int32)
    lengths = doc_lengths[0]
    starts = jnp.cumsum(lengths) - lengths
    resets = jnp.any(position[:, None] == starts[None, :], axis=1).astype(jnp.int32)
    stats = block_stats(log_rows, resets)
    log_cum, seg_count, carry_gain, weight_end, weight_start = stats
    weighted_values = head_scale(values, weight_end).astype(jnp.bfloat16)
    weighted_grads = head_scale(grads_in, weight_start).astype(jnp.bfloat16)
    local_state = product("li,ln->in", weighted_values, input_rows)
    local_adjoint = product("li,ln->in", weighted_grads, output_rows)
    gain_rows = jnp.broadcast_to(carry_gain[None, :, None, None], (1, head_count, head_dim, 1))
    shaped = (
        local_state.reshape(1, head_count, head_dim, state_width),
        local_adjoint.reshape(1, head_count, head_dim, state_width),
        gain_rows,
    )
    states_all = lax.all_to_all(shaped[0], SEQ, split_axis=1, concat_axis=0, tiled=True)
    adjoints_all = lax.all_to_all(shaped[1], SEQ, split_axis=1, concat_axis=0, tiled=True)
    gains_all = lax.all_to_all(shaped[2], SEQ, split_axis=1, concat_axis=0, tiled=True)
    anchor = jnp.zeros(states_all.shape[1:], jnp.float32)

    def advance(running, element):
        factor, addend = element
        return (factor * running + addend, running)

    unused_a, state_prefix = lax.scan(advance, anchor, (gains_all, states_all))
    unused_b, adjoint_prefix = lax.scan(advance, anchor, (gains_all, adjoints_all), reverse=True)
    state_back, adjoint_back = in_one_piece((state_prefix, adjoint_prefix), SEQ, 0, 1, 2)
    state_in = state_back.reshape(inner_width, state_width)
    adjoint_in = adjoint_back.reshape(inner_width, state_width)
    results = finish_block(
        values,
        input_rows,
        output_rows,
        grads_in,
        resets,
        skip_gain,
        stats,
        weighted_values,
        weighted_grads,
        state_in,
        adjoint_in,
    )
    mixed, values_grad, input_raw, output_raw, decay_raw, skip_part = results
    token_count = shards * row_count
    seq_count = lax.axis_size("dp")
    input_grad = input_raw * (1.0 / jnp.sqrt(jnp.float32(head_count * head_dim)))
    output_grad = output_raw * jnp.sqrt(
        jnp.float32(state_width) / jnp.float32(head_count * head_dim * token_count)
    )
    decay_grad = decay_raw * (1.0 / jnp.sqrt(jnp.float32(head_dim * token_count)))
    skip_total = one_axis_at_a_time(skip_part, DP_SEQ)
    skip_grad = skip_total / jnp.sqrt(jnp.float32(seq_count * token_count * head_dim))
    return (
        mixed[None],
        values_grad[None],
        input_grad[None],
        output_grad[None],
        decay_grad[None],
        skip_grad,
    )


def solution(mesh):
    finer = Mesh(mesh.devices.reshape(mesh.shape["dp"], 4, 4, 2), ("dp", "seq_0", "seq_1", "seq_2"))
    placed = (
        P("dp", SEQ, None),
        P("dp", SEQ, None),
        P("dp", SEQ, None),
        P("dp", None, SEQ),
        P("dp", None),
        P(),
        P("dp", SEQ, None),
    )
    return jax.shard_map(
        body,
        mesh=finer,
        in_specs=placed,
        out_specs=(
            P("dp", SEQ, None),
            P("dp", SEQ, None),
            P("dp", SEQ, None),
            P("dp", SEQ, None),
            P("dp", None, SEQ),
            P(),
        ),
        check_vma=False,
    )
```

profile of v0, /device:TPU:1, one launch (start us, length us, event | category | flops | bytes accessed | tf_op | source)
XLA Modules:
  0.0 180.9 jit_solution(5471237887130458574)
XLA Ops:
  5.5 8.6 %all-to-all-start = ((f32[1,32,64,1]{2,3,0,1:T(1,128)}), f32[1,32,64,1]{2,3,0,1:T(1,128)S(1)}, u32[]{:S(2)}, u32[]{:S(2)}) async-start(f32[1,32,64,1]{2,3,0,1:T(1,128)} %broadcast_in_dim.133), calls=%async_computation | async-start | bytes 32768 | tf_op jit(solution)/shard_map/all_to_all | solution.py:165
  15.6 1.3 copy.85
  17.0 1.3 copy.92
  27.2 1.3 convolution_bitcast_fusion.2
  28.7 1.3 convolution_bitcast_fusion.3
  31.7 1.8 fusion.82
  34.6 7.4 %all-to-all-start.2 = ((f32[1,32,64,128]{3,2,0,1:T(8,128)}), f32[1,32,64,128]{3,2,0,1:T(8,128)S(1)}, u32[]{:S(2)}, u32[]{:S(2)}) async-start(f32[1,32,64,128]{3,2,0,1:T(8,128)} %convolution_bitcast_fusion.2), calls=%async_computation.2 | async-start | bytes 2097152 | tf_op jit(solution)/shard_map/all_to_all | solution.py:164
  43.9 1.1 fusion.207
  47.2 3.5 %fusion.52 = (f32[4,128]{1,0:T(4,128)}, f32[4,128]{1,0:T(4,128)}, f32[128,128]{1,0:T(8,128)}, f32[128,128]{1,0:T(8,128)}, f32[4,128]{1,0:T(4,128)}, /*index=5*/f...) fusion(f32[4,128]{1,0:T(4,128)} %get-tuple-element.369, ...), kind=kOutput, calls=%fused_computation.97 | convolution fusion | flops 12443648 | bytes 2621440 | tf_op jit(solution)/shard_map/tgp,sgp->gts/dot_general | solution.py:32
  50.7 8.2 %all-to-all-done.2 = f32[1,32,64,128]{3,2,0,1:T(8,128)S(1)} async-done(((f32[1,32,64,128]{3,2,0,1:T(8,128)}), f32[1,32,64,128]{3,2,0,1:T(8,128)S(1)}, u32[]{:S(2)}, u32[]{:S(2)}) %all-to-all-start.2) | async-done | bytes 1048608 | tf_op jit(solution)/shard_map/all_to_all | solution.py:164
  58.9 4.5 %all-to-all-start.1 = ((f32[1,32,64,128]{3,2,0,1:T(8,128)}), f32[1,32,64,128]{3,2,0,1:T(8,128)}, u32[]{:S(2)}, u32[]{:S(2)}) async-start(f32[1,32,64,128]{3,2,0,1:T(8,128)} %convolution_bitcast_fusion.3), calls=%async_computation.1 | async-start | bytes 2097152 | tf_op jit(solution)/shard_map/all_to_all | solution.py:163
  63.5 3.1 %while.32 = (s32[]{:T(128)}, f32[1,64,128]{2,1,0:T(8,128)S(1)}, f32[32,1,64,128]{3,2,1,0:T(8,128)S(1)}, f32[32,1,64,1]{2,3,1,0:T(1,128)S(1)}, f32[32,1,64,128]{3...) while((s32[]{:T(128)}, f32[1,64,128]{2,1,0:T(8,128)S(1)}, ...), condition=%wide.region_7.8_spmd.clone, body=%wide.region_6.7_spmd.clone.sunk | while | flops 32772 | bytes 164736 | solution.py:173
  66.6 13.7 %all-to-all-done.1 = f32[1,32,64,128]{3,2,0,1:T(8,128)} async-done(((f32[1,32,64,128]{3,2,0,1:T(8,128)}), f32[1,32,64,128]{3,2,0,1:T(8,128)}, u32[]{:S(2)}, u32[]{:S(2)}) %all-to-all-start.1) | async-done | bytes 1048608 | tf_op jit(solution)/shard_map/all_to_all | solution.py:163
  80.4 27.6 %while.31 = (s32[]{:T(128)}, f32[1,64,128]{2,1,0:T(8,128)S(1)}, f32[32,1,64,128]{3,2,1,0:T(8,128)S(1)}, f32[32,1,64,1]{2,3,1,0:T(1,128)S(1)}, f32[32,1,64,128]{3,2,1,0:T(8,128)}, /*index=5*/s32[]{:T(128)}, s32[]{:T(128)}) while((s32[]{:T(128)}, f32[1,64,128]{2,1,0:T(8,128)S(1)}, f32[32,1,64,128]{3,2,1,0:T(8,128)S(1)}, ...), condition=%wide.region_5.6_spmd.clone, body=%wide.region_4.5_spmd.clone.sunk | while | flops 32771 | bytes 164716 | solution.py:172
  108.1 1.5 pad_maximum_fusion
  109.6 4.0 %all-to-all-start.3 = ((f32[32,1,128,128]{3,2,1,0:T(8,128)}), f32[32,1,128,128]{3,2,1,0:T(8,128)S(1)}, u32[]{:S(2)}, u32[]{:S(2)}) async-start(f32[32,1,128,128]{3,2,1,0:T(8,128)} %pad_maximum_fusion), calls=%async_computation.3 | async-start | bytes 4194304 | tf_op jit(solution)/shard_map/all_to_all | solution.py:20
  120.3 17.4 %psum.28 = f32[32]{0:T(128)S(1)} all-reduce(f32[32]{0:T(128)S(1)} %reduce_sum.308), channel_id=1, replica_groups=mesh['dp'=8,'seq_0'=4,'seq_1'=4,'seq_2'=2] {'dp'}, use_global_device_ids=true, to_apply=%region_39.40 | all-reduce | flops 32 | bytes 256 | tf_op jit(solution)/shard_map/psum | solution.py:28
  137.7 8.6 %psum.29 = f32[32]{0:T(128)S(1)} all-reduce(f32[32]{0:T(128)S(1)} %psum.28), channel_id=1, replica_groups=mesh['dp'=8,'seq_0'=4,'seq_1'=4,'seq_2'=2] {'seq_0'}, use_global_device_ids=true, to_apply=%region_40.41 | all-reduce | flops 32 | bytes 256 | tf_op jit(solution)/shard_map/psum | solution.py:28
  146.3 8.4 %psum.30 = f32[32]{0:T(128)S(1)} all-reduce(f32[32]{0:T(128)S(1)} %psum.29), channel_id=1, replica_groups=mesh['dp'=8,'seq_0'=4,'seq_1'=4,'seq_2'=2] {'seq_1'}, use_global_device_ids=true, to_apply=%region_41.42 | all-reduce | flops 32 | bytes 256 | tf_op jit(solution)/shard_map/psum | solution.py:28
  154.7 9.1 %psum.31 = f32[32]{0:T(128)S(1)} all-reduce(f32[32]{0:T(128)S(1)} %psum.30), channel_id=1, replica_groups=mesh['dp'=8,'seq_0'=4,'seq_1'=4,'seq_2'=2] {'seq_2'}, use_global_device_ids=true, to_apply=%region_42.43 | all-reduce | flops 32 | bytes 256 | tf_op jit(solution)/shard_map/psum | solution.py:28
  163.9 1.1 fusion.84
  165.0 1.6 constant_dynamic-update-slice_fusion
  166.6 1.2 fusion.184
  168.3 1.1 add_convert_fusion
  (368 shorter events, 70.2 us)
Async XLA Ops:
  0.6 18.8 %copy-start = (bf16[1,128,128]{2,1,0:T(8,128)(2,1)S(1)}, bf16[1,128,128]{2,1,0:T(8,128)(2,1)}, u32[]{:S(2)}) copy-start(bf16[1,128,128]{2,1,0:T(8,128)(2,1)} %param.14) | copy-start | bytes 98308
  5.5 29.1 %all-to-all-start = ((f32[1,32,64,1]{2,3,0,1:T(1,128)}), f32[1,32,64,1]{2,3,0,1:T(1,128)S(1)}, u32[]{:S(2)}, u32[]{:S(2)}) async-start(f32[1,32,64,1]{2,3,0,1:T(1,128)} %broadcast_in_dim.133), calls=%async_computation | async-start | bytes 32768 | tf_op jit(solution)/shard_map/all_to_all | solution.py:165
  14.7 5.8 %copy-start.26 = (f32[4,128]{1,0:T(4,128)}, f32[4,128]{1,0:T(4,128)S(1)}, u32[]{:S(2)}) copy-start(f32[4,128]{1,0:T(4,128)S(1)} %get-tuple-element.370) | copy-start | bytes 6148
  14.7 7.9 %copy-start.27 = (f32[4,128]{1,0:T(4,128)}, f32[4,128]{1,0:T(4,128)S(1)}, u32[]{:S(2)}) copy-start(f32[4,128]{1,0:T(4,128)S(1)} %get-tuple-element.371) | copy-start | bytes 6148
  14.7 9.4 %copy-start.28 = (f32[4,128]{1,0:T(4,128)}, f32[4,128]{1,0:T(4,128)S(1)}, u32[]{:S(2)}) copy-start(f32[4,128]{1,0:T(4,128)S(1)} %get-tuple-element.372) | copy-start | bytes 6148
  14.7 10.9 %copy-start.29 = (f32[4,128]{1,0:T(4,128)}, f32[4,128]{1,0:T(4,128)S(1)}, u32[]{:S(2)}) copy-start(f32[4,128]{1,0:T(4,128)S(1)} %get-tuple-element.373) | copy-start | bytes 6148
  14.7 15.5 %copy-start.30 = (f32[4,128]{1,0:T(4,128)}, f32[4,128]{1,0:T(4,128)S(1)}, u32[]{:S(2)}) copy-start(f32[4,128]{1,0:T(4,128)S(1)} %get-tuple-element.374) | copy-start | bytes 6148
  14.7 16.0 %copy-start.31 = (f32[4,128]{1,0:T(4,128)}, f32[4,128]{1,0:T(4,128)S(1)}, u32[]{:S(2)}) copy-start(f32[4,128]{1,0:T(4,128)S(1)} %get-tuple-element.375) | copy-start | bytes 6148
  14.8 16.6 %copy-start.32 = (f32[4,128]{1,0:T(4,128)}, f32[4,128]{1,0:T(4,128)S(1)}, u32[]{:S(2)}) copy-start(f32[4,128]{1,0:T(4,128)S(1)} %get-tuple-element.376) | copy-start | bytes 6148
  14.8 12.1 %copy-start.21 = (f32[32]{0:T(128)}, f32[32]{0:T(128)S(1)}, u32[]{:S(2)}) copy-start(f32[32]{0:T(128)S(1)} %slice_bitcast_fusion) | copy-start | bytes 388
  18.7 11.2 %copy-start.13 = (bf16[128,256]{0,1:T(8,128)(2,1)}, bf16[128,256]{0,1:T(8,128)(2,1)S(1)}, u32[]{:S(2)}) copy-start(bf16[128,256]{0,1:T(8,128)(2,1)S(1)} %get-tuple-element.354) | copy-start | bytes 196612
  18.7 13.0 %copy-start.19 = (bf16[128,256]{0,1:T(8,128)(2,1)}, bf16[128,256]{0,1:T(8,128)(2,1)S(1)}, u32[]{:S(2)}) copy-start(bf16[128,256]{0,1:T(8,128)(2,1)S(1)} %get-tuple-element.349) | copy-start | bytes 196612
  19.4 10.8 %copy-start.16 = (bf16[128,256]{0,1:T(8,128)(2,1)}, bf16[128,256]{0,1:T(8,128)(2,1)S(1)}, u32[]{:S(2)}) copy-start(bf16[128,256]{0,1:T(8,128)(2,1)S(1)} %get-tuple-element.362) | copy-start | bytes 196612
  19.4 11.4 %copy-start.15 = (bf16[128,256]{0,1:T(8,128)(2,1)}, bf16[128,256]{0,1:T(8,128)(2,1)S(1)}, u32[]{:S(2)}) copy-start(bf16[128,256]{0,1:T(8,128)(2,1)S(1)} %get-tuple-element.363) | copy-start | bytes 196612
  19.4 12.0 %copy-start.14 = (bf16[128,256]{0,1:T(8,128)(2,1)}, bf16[128,256]{0,1:T(8,128)(2,1)S(1)}, u32[]{:S(2)}) copy-start(bf16[128,256]{0,1:T(8,128)(2,1)S(1)} %get-tuple-element.364) | copy-start | bytes 196612
  19.5 11.8 %copy-start.20 = (f32[128,128]{1,0:T(8,128)}, f32[128,128]{1,0:T(8,128)S(1)}, u32[]{:S(2)}) copy-start(f32[128,128]{1,0:T(8,128)S(1)} %fusion.177) | copy-start | bytes 196612
  34.6 24.3 %all-to-all-start.2 = ((f32[1,32,64,128]{3,2,0,1:T(8,128)}), f32[1,32,64,128]{3,2,0,1:T(8,128)S(1)}, u32[]{:S(2)}, u32[]{:S(2)}) async-start(f32[1,32,64,128]{3,2,0,1:T(8,128)} %convolution_bitcast_fusion.2), calls=%async_computation.2 | async-start | bytes 2097152 | tf_op jit(solution)/shard_map/all_to_all | solution.py:164
  58.9 21.4 %all-to-all-start.1 = ((f32[1,32,64,128]{3,2,0,1:T(8,128)}), f32[1,32,64,128]{3,2,0,1:T(8,128)}, u32[]{:S(2)}, u32[]{:S(2)}) async-start(f32[1,32,64,128]{3,2,0,1:T(8,128)} %convolution_bitcast_fusion.3), calls=%async_computation.1 | async-start | bytes 2097152 | tf_op jit(solution)/shard_map/all_to_all | solution.py:163
  109.6 4.1 %copy-start.17 = (f32[4,128,64]{1,2,0:T(8,128)S(1)}, f32[4,128,64]{1,2,0:T(8,128)}, u32[]{:S(2)}) copy-start(f32[4,128,64]{1,2,0:T(8,128)} %fusion.78) | copy-start | bytes 393220
  109.6 4.7 %copy-start.34 = (f32[32]{0:T(128)S(1)}, f32[32]{0:T(128)}, u32[]{:S(2)}) copy-start(f32[32]{0:T(128)} %param.18) | copy-start | bytes 388
  109.6 9.8 %copy-start.25 = (f32[4,128]{1,0:T(4,128)S(1)}, f32[4,128]{1,0:T(4,128)}, u32[]{:S(2)}) copy-start(f32[4,128]{1,0:T(4,128)} %get-tuple-element.325) | copy-start | bytes 6148
  109.6 54.3 %copy-start.18 = (bf16[128,256]{0,1:T(8,128)(2,1)S(1)}, bf16[128,256]{0,1:T(8,128)(2,1)}, u32[]{:S(2)}) copy-start(bf16[128,256]{0,1:T(8,128)(2,1)} %get-tuple-element.357) | copy-start | bytes 196612
  109.6 54.3 %copy-start.24 = (f32[4,128]{1,0:T(4,128)S(1)}, f32[4,128]{1,0:T(4,128)}, u32[]{:S(2)}) copy-start(f32[4,128]{1,0:T(4,128)} %get-tuple-element.369) | copy-start | bytes 6148
  109.6 62.7 %all-to-all-start.3 = ((f32[32,1,128,128]{3,2,1,0:T(8,128)}), f32[32,1,128,128]{3,2,1,0:T(8,128)S(1)}, u32[]{:S(2)}, u32[]{:S(2)}) async-start(f32[32,1,128,128]{3,2,1,0:T(8,128)} %pad_maximum_fusion), calls=%async_computation.3 | async-start | bytes 4194304 | tf_op jit(solution)/shard_map/all_to_all | solution.py:20
  (16 other events, 38.4 us)
where the time goes:
time: 184 us; the launch traced here: 181 us
  other arithmetic  47.6 us (26%)
  blocking collectives  43.6 us (24%)
  matrix products  25.2 us (14%)
  starting transfers between devices  24.5 us (13%)
  waiting for transfers between devices  22 us (12%)
  local copies, waits for them, and re-layouts  15.6 us (8%)
  between operations  1.95 us (1%)
    psum x4, blocking collectives, one_axis_at_a_time(): return functools.reduce(lax.psum, axes, x)  43.6 us
    add x64, other arithmetic, advance(): return (factor * running + addend, running)  29.5 us
    dot_general x33, matrix products, product(): jnp.einsum(form, left_side, right_side, preferred_element_type=jnp.float32)  25.2 us
    all_to_all x1, waiting for transfers between devices, body(): lax.all_to_all(shaped[0], SEQ, split_axis=1, concat_axis=0, tiled=True)  13.7 us
    unnamed x90, local copies, waits for them, and re-layouts  9.78 us
    all_to_all x1, starting transfers between devices, body(): lax.all_to_all(shaped[2], SEQ, split_axis=1, concat_axis=0, tiled=True)  8.58 us
    all_to_all x1, waiting for transfers between devices, body(): lax.all_to_all(shaped[1], SEQ, split_axis=1, concat_axis=0, tiled=True)  8.21 us
    all_to_all x1, starting transfers between devices, body(): lax.all_to_all(shaped[1], SEQ, split_axis=1, concat_axis=0, tiled=True)  7.4 us
  transfers between devices with their start and end apart: 4, of which 2 were waited for; matrix products, arithmetic and copies ran while one was open for 25% of the time, Pallas kernels for 0%

commit v1 on v0

--- a/solution.py
+++ b/solution.py
@@ -7,6 +7,13 @@
 
 SEQ = ("seq_0", "seq_1", "seq_2")
 DP_SEQ = ("dp", "seq_0", "seq_1", "seq_2")
+
+
+def swap_blocks(x, axis, split, join):
+    size = lax.axis_size(axis)
+    tiles = jnp.stack(jnp.split(x, size, axis=split), axis=0)
+    tiles = lax.all_to_all(tiles, axis, split_axis=0, concat_axis=0)
+    return jnp.concatenate(tiles, axis=join)
 
 
 def in_one_piece(arrays, axis, split_dim, concat_dim, along):
@@ -161,7 +168,7 @@
         gain_rows,
     )
     states_all = lax.all_to_all(shaped[0], SEQ, split_axis=1, concat_axis=0, tiled=True)
-    adjoints_all = lax.all_to_all(shaped[1], SEQ, split_axis=1, concat_axis=0, tiled=True)
+    adjoints_all = swap_blocks(shaped[1], SEQ, 1, 0)
     gains_all = lax.all_to_all(shaped[2], SEQ, split_axis=1, concat_axis=0, tiled=True)
     anchor = jnp.zeros(states_all.shape[1:], jnp.float32)
 

time: 184 us -> 188 us (1.022)
  matrix products: 25.2 us -> 27.2 us
    dot_general x33, matrix products: 25.2 us -> 27.2 us  [product(): jnp.einsum(form, left_side, right_side, preferred_element_type=jnp.float32)]
    unnamed x90 -> x137, local copies, waits for them, and re-layouts: 9.78 us -> 10.8 us
where the time goes in v1:
time: 188 us; the launch traced here: 185 us
  other arithmetic  47.6 us (25%)
  blocking collectives  43.7 us (23%)
  matrix products  27.2 us (14%)
  starting transfers between devices  24.5 us (13%)
  waiting for transfers between devices  21.9 us (12%)
  local copies, waits for them, and re-layouts  16.6 us (9%)
  between operations  2.29 us (1%)
    psum x4, blocking collectives, one_axis_at_a_time(): return functools.reduce(lax.psum, axes, x)  43.7 us
    add x64, other arithmetic, advance(): return (factor * running + addend, running)  29.5 us
    dot_general x33, matrix products, product(): jnp.einsum(form, left_side, right_side, preferred_element_type=jnp.float32)  27.2 us
    all_to_all x1, waiting for transfers between devices, body(): lax.all_to_all(shaped[0], SEQ, split_axis=1, concat_axis=0, tiled=True)  13.7 us
    unnamed x137, local copies, waits for them, and re-layouts  10.8 us
    all_to_all x1, starting transfers between devices, body(): lax.all_to_all(shaped[2], SEQ, split_axis=1, concat_axis=0, tiled=True)  8.58 us
    all_to_all x1, waiting for transfers between devices, swap_blocks(): tiles = lax.all_to_all(tiles, axis, split_axis=0, concat_axis=0)  8.19 us
    all_to_all x1, starting transfers between devices, swap_blocks(): tiles = lax.all_to_all(tiles, axis, split_axis=0, concat_axis=0)  7.41 us
  transfers between devices with their start and end apart: 4, of which 2 were waited for; matrix products, arithmetic and copies ran while one was open for 25% of the time, Pallas kernels for 0%

profile of v1, /device:TPU:1, one launch (start us, length us, event | category | flops | bytes accessed | tf_op | source)
XLA Modules:
  0.0 184.5 jit_solution(3556942553266807134)
XLA Ops:
  6.1 8.6 %all-to-all-start = ((f32[1,32,64,1]{2,3,0,1:T(1,128)}), f32[1,32,64,1]{2,3,0,1:T(1,128)S(1)}, u32[]{:S(2)}, u32[]{:S(2)}) async-start(f32[1,32,64,1]{2,3,0,1:T(1,128)} %broadcast_in_dim.133), calls=%async_computation | async-start | bytes 32768 | tf_op jit(solution)/shard_map/all_to_all | solution.py:172
  16.2 1.3 copy.82
  17.6 1.3 copy.89
  32.0 1.3 convolution_bitcast_fusion.3
  38.0 7.4 %all-to-all-start.2 = ((f32[32,1,1,64,128]{4,3,2,1,0:T(8,128)}), f32[32,1,1,64,128]{4,3,2,1,0:T(8,128)S(1)}, u32[]{:S(2)}, u32[]{:S(2)}) async-start(f32[32,1,1,64,128]{4,3,2,1,0:T(8,128)} %copy-done.11), calls=%async_computation.2 | async-start | bytes 2097152 | tf_op jit(solution)/shard_map/all_to_all | solution.py:15
  47.3 1.1 fusion.207
  48.4 1.1 fusion.206
  49.5 1.1 fusion.205
  50.6 3.5 %fusion.52 = (f32[4,128]{1,0:T(4,128)}, f32[4,128]{1,0:T(4,128)}, f32[128,128]{1,0:T(8,128)}, f32[128,128]{1,0:T(8,128)}, f32[4,128]{1,0:T(4,128)}, /*index=5*/f...) fusion(f32[4,128]{1,0:T(4,128)} %get-tuple-element.369, ...), kind=kOutput, calls=%fused_computation.97 | convolution fusion | flops 12443648 | bytes 2621440 | tf_op jit(solution)/shard_map/tgp,sgp->gts/dot_general | solution.py:39
  54.1 8.2 %all-to-all-done.2 = f32[32,1,1,64,128]{4,3,2,1,0:T(8,128)S(1)} async-done(((f32[32,1,1,64,128]{4,3,2,1,0:T(8,128)}), f32[32,1,1,64,128]{4,3,2,1,0:T(8,128)S(1)}, u32[]{:S(2)}, u32[]{:S(2)}) %all-to-all-start.2) | async-done | bytes 1048608 | tf_op jit(solution)/shard_map/all_to_all | solution.py:15
  62.3 4.5 %all-to-all-start.1 = ((f32[1,32,64,128]{3,2,0,1:T(8,128)}), f32[1,32,64,128]{3,2,0,1:T(8,128)}, u32[]{:S(2)}, u32[]{:S(2)}) async-start(f32[1,32,64,128]{3,2,0,1:T(8,128)} %convolution_bitcast_fusion.3), calls=%async_computation.1 | async-start | bytes 2097152 | tf_op jit(solution)/shard_map/all_to_all | solution.py:170
  66.9 3.1 %while.32 = (s32[]{:T(128)}, f32[1,64,128]{2,1,0:T(8,128)S(1)}, f32[32,1,64,128]{3,2,1,0:T(8,128)S(1)}, f32[32,1,64,1]{2,3,1,0:T(1,128)S(1)}, f32[32,1,64,128]{3...) while((s32[]{:T(128)}, f32[1,64,128]{2,1,0:T(8,128)S(1)}, ...), condition=%wide.region_7.8_spmd.clone, body=%wide.region_6.7_spmd.clone.sunk | while | flops 32772 | bytes 164736 | solution.py:180
  70.0 13.7 %all-to-all-done.1 = f32[1,32,64,128]{3,2,0,1:T(8,128)} async-done(((f32[1,32,64,128]{3,2,0,1:T(8,128)}), f32[1,32,64,128]{3,2,0,1:T(8,128)}, u32[]{:S(2)}, u32[]{:S(2)}) %all-to-all-start.1) | async-done | bytes 1048608 | tf_op jit(solution)/shard_map/all_to_all | solution.py:170
  83.9 27.6 %while.31 = (s32[]{:T(128)}, f32[1,64,128]{2,1,0:T(8,128)S(1)}, f32[32,1,64,128]{3,2,1,0:T(8,128)S(1)}, f32[32,1,64,1]{2,3,1,0:T(1,128)S(1)}, f32[32,1,64,128]{3,2,1,0:T(8,128)}, /*index=5*/s32[]{:T(128)}, s32[]{:T(128)}) while((s32[]{:T(128)}, f32[1,64,128]{2,1,0:T(8,128)S(1)}, f32[32,1,64,128]{3,2,1,0:T(8,128)S(1)}, ...), condition=%wide.region_5.6_spmd.clone, body=%wide.region_4.5_spmd.clone.sunk | while | flops 32771 | bytes 164716 | solution.py:179
  111.5 1.5 pad_maximum_fusion
  113.0 4.0 %all-to-all-start.3 = ((f32[32,1,128,128]{3,2,1,0:T(8,128)}), f32[32,1,128,128]{3,2,1,0:T(8,128)S(1)}, u32[]{:S(2)}, u32[]{:S(2)}) async-start(f32[32,1,128,128]{3,2,1,0:T(8,128)} %pad_maximum_fusion), calls=%async_computation.3 | async-start | bytes 4194304 | tf_op jit(solution)/shard_map/all_to_all | solution.py:27
  123.7 17.4 %psum.28 = f32[32]{0:T(128)S(1)} all-reduce(f32[32]{0:T(128)S(1)} %reduce_sum.308), channel_id=1, replica_groups=mesh['dp'=8,'seq_0'=4,'seq_1'=4,'seq_2'=2] {'dp'}, use_global_device_ids=true, to_apply=%region_39.40 | all-reduce | flops 32 | bytes 256 | tf_op jit(solution)/shard_map/psum | solution.py:35
  141.1 8.6 %psum.29 = f32[32]{0:T(128)S(1)} all-reduce(f32[32]{0:T(128)S(1)} %psum.28), channel_id=1, replica_groups=mesh['dp'=8,'seq_0'=4,'seq_1'=4,'seq_2'=2] {'seq_0'}, use_global_device_ids=true, to_apply=%region_40.41 | all-reduce | flops 32 | bytes 256 | tf_op jit(solution)/shard_map/psum | solution.py:35
  149.7 8.4 %psum.30 = f32[32]{0:T(128)S(1)} all-reduce(f32[32]{0:T(128)S(1)} %psum.29), channel_id=1, replica_groups=mesh['dp'=8,'seq_0'=4,'seq_1'=4,'seq_2'=2] {'seq_1'}, use_global_device_ids=true, to_apply=%region_41.42 | all-reduce | flops 32 | bytes 256 | tf_op jit(solution)/shard_map/psum | solution.py:35
  158.1 9.3 %psum.31 = f32[32]{0:T(128)S(1)} all-reduce(f32[32]{0:T(128)S(1)} %psum.30), channel_id=1, replica_groups=mesh['dp'=8,'seq_0'=4,'seq_1'=4,'seq_2'=2] {'seq_2'}, use_global_device_ids=true, to_apply=%region_42.43 | all-reduce | flops 32 | bytes 256 | tf_op jit(solution)/shard_map/psum | solution.py:35
  167.4 1.1 fusion.84
  168.6 1.6 constant_dynamic-update-slice_fusion
  170.2 1.2 fusion.184
  171.9 1.1 add_convert_fusion
  (416 shorter events, 74.2 us)
Async XLA Ops:
  0.6 19.3 %copy-start = (bf16[1,128,128]{2,1,0:T(8,128)(2,1)S(1)}, bf16[1,128,128]{2,1,0:T(8,128)(2,1)}, u32[]{:S(2)}) copy-start(bf16[1,128,128]{2,1,0:T(8,128)(2,1)} %param.14) | copy-start | bytes 98308
  6.1 31.9 %all-to-all-start = ((f32[1,32,64,1]{2,3,0,1:T(1,128)}), f32[1,32,64,1]{2,3,0,1:T(1,128)S(1)}, u32[]{:S(2)}, u32[]{:S(2)}) async-start(f32[1,32,64,1]{2,3,0,1:T(1,128)} %broadcast_in_dim.133), calls=%async_computation | async-start | bytes 32768 | tf_op jit(solution)/shard_map/all_to_all | solution.py:172
  15.3 5.8 %copy-start.33 = (f32[4,128]{1,0:T(4,128)}, f32[4,128]{1,0:T(4,128)S(1)}, u32[]{:S(2)}) copy-start(f32[4,128]{1,0:T(4,128)S(1)} %get-tuple-element.370) | copy-start | bytes 6148
  15.3 8.6 %copy-start.34 = (f32[4,128]{1,0:T(4,128)}, f32[4,128]{1,0:T(4,128)S(1)}, u32[]{:S(2)}) copy-start(f32[4,128]{1,0:T(4,128)S(1)} %get-tuple-element.371) | copy-start | bytes 6148
  15.3 11.3 %copy-start.35 = (f32[4,128]{1,0:T(4,128)}, f32[4,128]{1,0:T(4,128)S(1)}, u32[]{:S(2)}) copy-start(f32[4,128]{1,0:T(4,128)S(1)} %get-tuple-element.372) | copy-start | bytes 6148
  15.3 14.1 %copy-start.36 = (f32[4,128]{1,0:T(4,128)}, f32[4,128]{1,0:T(4,128)S(1)}, u32[]{:S(2)}) copy-start(f32[4,128]{1,0:T(4,128)S(1)} %get-tuple-element.373) | copy-start | bytes 6148
  15.3 18.3 %copy-start.37 = (f32[4,128]{1,0:T(4,128)}, f32[4,128]{1,0:T(4,128)S(1)}, u32[]{:S(2)}) copy-start(f32[4,128]{1,0:T(4,128)S(1)} %get-tuple-element.374) | copy-start | bytes 6148
  15.3 18.8 %copy-start.38 = (f32[4,128]{1,0:T(4,128)}, f32[4,128]{1,0:T(4,128)S(1)}, u32[]{:S(2)}) copy-start(f32[4,128]{1,0:T(4,128)S(1)} %get-tuple-element.375) | copy-start | bytes 6148
  15.3 19.4 %copy-start.39 = (f32[4,128]{1,0:T(4,128)}, f32[4,128]{1,0:T(4,128)S(1)}, u32[]{:S(2)}) copy-start(f32[4,128]{1,0:T(4,128)S(1)} %get-tuple-element.376) | copy-start | bytes 6148
  15.3 15.9 %copy-start.29 = (f32[32]{0:T(128)}, f32[32]{0:T(128)S(1)}, u32[]{:S(2)}) copy-start(f32[32]{0:T(128)S(1)} %slice_bitcast_fusion.32) | copy-start | bytes 388
  19.3 14.0 %copy-start.14 = (bf16[128,256]{0,1:T(8,128)(2,1)}, bf16[128,256]{0,1:T(8,128)(2,1)S(1)}, u32[]{:S(2)}) copy-start(bf16[128,256]{0,1:T(8,128)(2,1)S(1)} %get-tuple-element.354) | copy-start | bytes 196612
  19.3 16.3 %copy-start.26 = (bf16[128,256]{0,1:T(8,128)(2,1)}, bf16[128,256]{0,1:T(8,128)(2,1)S(1)}, u32[]{:S(2)}) copy-start(bf16[128,256]{0,1:T(8,128)(2,1)S(1)} %get-tuple-element.349) | copy-start | bytes 196612
  20.0 13.6 %copy-start.17 = (bf16[128,256]{0,1:T(8,128)(2,1)}, bf16[128,256]{0,1:T(8,128)(2,1)S(1)}, u32[]{:S(2)}) copy-start(bf16[128,256]{0,1:T(8,128)(2,1)S(1)} %get-tuple-element.362) | copy-start | bytes 196612
  20.0 14.2 %copy-start.16 = (bf16[128,256]{0,1:T(8,128)(2,1)}, bf16[128,256]{0,1:T(8,128)(2,1)S(1)}, u32[]{:S(2)}) copy-start(bf16[128,256]{0,1:T(8,128)(2,1)S(1)} %get-tuple-element.363) | copy-start | bytes 196612
  20.0 14.8 %copy-start.15 = (bf16[128,256]{0,1:T(8,128)(2,1)}, bf16[128,256]{0,1:T(8,128)(2,1)S(1)}, u32[]{:S(2)}) copy-start(bf16[128,256]{0,1:T(8,128)(2,1)S(1)} %get-tuple-element.364) | copy-start | bytes 196612
  20.1 14.6 %copy-start.27 = (f32[128,128]{1,0:T(8,128)}, f32[128,128]{1,0:T(8,128)S(1)}, u32[]{:S(2)}) copy-start(f32[128,128]{1,0:T(8,128)S(1)} %fusion.177) | copy-start | bytes 196612
  38.0 24.3 %all-to-all-start.2 = ((f32[32,1,1,64,128]{4,3,2,1,0:T(8,128)}), f32[32,1,1,64,128]{4,3,2,1,0:T(8,128)S(1)}, u32[]{:S(2)}, u32[]{:S(2)}) async-start(f32[32,1,1,64,128]{4,3,2,1,0:T(8,128)} %copy-done.11), calls=%async_computation.2 | async-start | bytes 2097152 | tf_op jit(solution)/shard_map/all_to_all | solution.py:15
  62.3 21.4 %all-to-all-start.1 = ((f32[1,32,64,128]{3,2,0,1:T(8,128)}), f32[1,32,64,128]{3,2,0,1:T(8,128)}, u32[]{:S(2)}, u32[]{:S(2)}) async-start(f32[1,32,64,128]{3,2,0,1:T(8,128)} %convolution_bitcast_fusion.3), calls=%async_computation.1 | async-start | bytes 2097152 | tf_op jit(solution)/shard_map/all_to_all | solution.py:170
  113.0 4.1 %copy-start.18 = (f32[4,128,64]{1,2,0:T(8,128)S(1)}, f32[4,128,64]{1,2,0:T(8,128)}, u32[]{:S(2)}) copy-start(f32[4,128,64]{1,2,0:T(8,128)} %fusion.78) | copy-start | bytes 393220
  113.0 4.7 %copy-start.42 = (f32[32]{0:T(128)S(1)}, f32[32]{0:T(128)}, u32[]{:S(2)}) copy-start(f32[32]{0:T(128)} %param.18) | copy-start | bytes 388
  113.0 9.8 %copy-start.40 = (f32[4,128]{1,0:T(4,128)S(1)}, f32[4,128]{1,0:T(4,128)}, u32[]{:S(2)}) copy-start(f32[4,128]{1,0:T(4,128)} %get-tuple-element.325) | copy-start | bytes 6148
  113.0 54.5 %copy-start.25 = (bf16[128,256]{0,1:T(8,128)(2,1)S(1)}, bf16[128,256]{0,1:T(8,128)(2,1)}, u32[]{:S(2)}) copy-start(bf16[128,256]{0,1:T(8,128)(2,1)} %get-tuple-element.357) | copy-start | bytes 196612
  113.0 54.5 %copy-start.32 = (f32[4,128]{1,0:T(4,128)S(1)}, f32[4,128]{1,0:T(4,128)}, u32[]{:S(2)}) copy-start(f32[4,128]{1,0:T(4,128)} %get-tuple-element.369) | copy-start | bytes 6148
  113.0 62.8 %all-to-all-start.3 = ((f32[32,1,128,128]{3,2,1,0:T(8,128)}), f32[32,1,128,128]{3,2,1,0:T(8,128)S(1)}, u32[]{:S(2)}, u32[]{:S(2)}) async-start(f32[32,1,128,128]{3,2,1,0:T(8,128)} %pad_maximum_fusion), calls=%async_computation.3 | async-start | bytes 4194304 | tf_op jit(solution)/shard_map/all_to_all | solution.py:27
  (24 other events, 52.3 us)
